TPU v7x, 512 devices: a whole 4x4x16 slice. The times are simulated.
512 devices in a mesh: fsdp: 32 (over x, z_hi, core), ctx: 16 (over y, z_lo).
Axes of the slice: x: 4, y: 4, z: 16 (z_hi: 4, z_lo: 4; z = z_hi * 4 + z_lo), core: 2. Of those that a mesh axis runs over, the one named last changes fastest.
Arguments:
- features: bfloat16 [3, 16384, 8192], P(None, 'ctx', 'fsdp'), may hold values from -6 to 6
- short_taps: float32 [3, 3, 8192], P(None, None, 'fsdp'), may hold values from -3.5 to 3.5
- decay_rates: float32 [512, 16], P('fsdp'), may hold values from 1.5258789e-05 to 0.1
- mode_gains: float32 [512, 16], P('fsdp'), may hold values from -2.5 to 2.5
- cotangent: bfloat16 [16384, 8192], P('ctx', 'fsdp'), may hold values from -6 to 6
Outputs:
- mixer_output: bfloat16 [16384, 8192], P('ctx', 'fsdp')
- feature_grads: bfloat16 [3, 16384, 8192], P(None, 'ctx', 'fsdp')
- gain_grads: float32 [512, 16], P('fsdp')
- rate_grads: float32 [512, 16], P('fsdp')
All inputs are finite; a program needn't handle non-finite values.
Results may differ from a plain program's by a relative error of at most 0.0048.
Values may be sent and summed in bfloat16 or wider, within the bound.
A program may use at most 64 MiB of HBM per device.

v0:
```python
import jax
import jax.numpy as jnp
from jax import lax
from jax.sharding import PartitionSpec as P

precise = lax.Precision.HIGHEST
threepass = lax.Precision.HIGH


def passed_along(value, axis, steps):
    count = lax.axis_size(axis)
    leading, last = (max(0, -steps), min(count, count - steps))
    return lax.ppermute(value, axis, [(source, source + steps) for source in range(leading, last)])


def diagonal_sums(gram_acc):
    group_count, block_len, width_same = gram_acc.shape
    flipped = jnp.flip(gram_acc, axis=2)
    padded = jnp.concatenate([flipped, jnp.zeros_like(flipped)], axis=2)
    flattened = padded.reshape(group_count, 2 * block_len * block_len)[
        :, : block_len * (2 * block_len - 1)
    ]
    sheared = flattened.reshape(group_count, block_len, 2 * block_len - 1)
    return jnp.sum(sheared, axis=1)[:, block_len - 1 :]


def short_conv(taps_table, row_data, tokens, rim_rows, forward):
    summed = jnp.zeros((3, tokens, row_data.shape[2]), jnp.float32)
    for offset in range(taps_table.shape[1]):
        start_row = rim_rows - offset if forward else offset
        summed = (
            summed + taps_table[:, offset, None, :] * row_data[:, start_row : start_row + tokens, :]
        )
    return summed


def per_device(features, short_taps, decay_rates, mode_gains, cotangent):
    tokens = features.shape[1]
    channels = features.shape[2]
    group_count = decay_rates.shape[0]
    order_count = decay_rates.shape[1]
    members = channels // group_count
    rim_rows = short_taps.shape[1] - 1
    block_len = 128
    block_count = tokens // block_len
    ctx_count = lax.axis_size("ctx")
    ctx_index = lax.axis_index("ctx")
    earlier_rows = passed_along(features[:, tokens - rim_rows :, :], "ctx", 1)
    extended = jnp.concatenate([earlier_rows, features], axis=1)
    shaped = short_conv(short_taps, extended, tokens, rim_rows, True)
    query_part, key_part, value_part = (shaped[0], shaped[1], shaped[2])
    product = (key_part * value_part).astype(jnp.bfloat16)
    adjoint = cotangent * query_part
    grouped_z = product.reshape(tokens, group_count, members)
    grouped_e = adjoint.reshape(tokens, group_count, members)
    mode_coefs = mode_gains * jnp.sqrt(2.0 * decay_rates)
    rate_axis = decay_rates[:, :, None]
    positions = jnp.arange(tokens, dtype=jnp.float32)[None, None, :]
    decay_from = jnp.exp(-rate_axis * positions)
    end_tables = jnp.stack([jnp.flip(decay_from, 2), -jnp.flip(positions * decay_from, 2)])
    end_states = jnp.einsum(
        "kgns,sgm->kngm", end_tables, grouped_z.astype(jnp.float32), precision=threepass
    )
    start_state = jnp.einsum("gnt,tgm->ngm", decay_from, grouped_e, precision=precise)
    local_states = jnp.stack([end_states[0], end_states[1], start_state]).reshape(
        3, order_count, channels
    )
    rate_cols = jnp.repeat(decay_rates.T, members, axis=1)
    everyone = lax.all_gather(local_states[None], "ctx", axis=0, tiled=True)
    device_ids = jnp.arange(ctx_count, dtype=jnp.int32)
    ahead_steps = (ctx_index - 1 - device_ids).astype(jnp.float32)[:, None, None]
    behind_steps = (device_ids - ctx_index - 1).astype(jnp.float32)[:, None, None]
    ahead_weight = jnp.where(
        ahead_steps >= 0, jnp.exp(-rate_cols[None] * (tokens * jnp.maximum(ahead_steps, 0.0))), 0.0
    )
    behind_weight = jnp.where(
        behind_steps >= 0,
        jnp.exp(-rate_cols[None] * (tokens * jnp.maximum(behind_steps, 0.0))),
        0.0,
    )
    prev_state = jnp.sum(ahead_weight * everyone[:, 0], axis=0)
    prev_lagged = jnp.sum(
        ahead_weight * (everyone[:, 1] - tokens * ahead_steps * everyone[:, 0]), axis=0
    )
    next_state = jnp.sum(behind_weight * everyone[:, 2], axis=0)
    lag_axis = jnp.arange(block_len, dtype=jnp.float32)[None, None, :]
    block_pow = jnp.exp(-rate_axis * lag_axis)
    block_after = block_pow * jnp.exp(-rate_axis)
    block_moments = jnp.stack([block_after, (lag_axis + 1.0) * block_after])
    coef_after = mode_coefs[:, :, None] * block_after
    block_ends = jnp.stack([jnp.flip(block_pow, 2), -jnp.flip(lag_axis * block_pow, 2)])
    coef_tail = mode_coefs[:, :, None] * jnp.flip(block_after, 2)
    block_span = jnp.exp(-decay_rates * block_len).T[:, :, None]
    filter_taps = jnp.sum(mode_coefs[:, :, None] * block_pow, axis=1)
    lag_index = (
        jnp.arange(block_len, dtype=jnp.int32)[:, None]
        - jnp.arange(block_len, dtype=jnp.int32)[None, :]
    )
    toeplitz = jnp.where(lag_index[None] >= 0, filter_taps[:, jnp.maximum(lag_index, 0)], 0.0)
    z_blocks = grouped_z.reshape(block_count, block_len, group_count, members)
    e_blocks = grouped_e.reshape(block_count, block_len, group_count, members)

    def forward_block(carried_in, inputs):
        mode_state, lagged, first_acc, lag_acc, gram_acc = carried_in
        z_block, e_block = inputs
        z_wide = z_block.astype(jnp.float32)
        inside_part = jnp.einsum("gts,sgm->tgm", toeplitz, z_wide, precision=threepass)
        carried = jnp.einsum("gnt,ngm->tgm", coef_after, mode_state, precision=precise)
        moments = jnp.einsum("kgnt,tgm->kngm", block_moments, e_block, precision=precise)
        first_acc = first_acc + jnp.sum(moments[0] * mode_state, axis=2)
        lag_acc = lag_acc + jnp.sum(moments[0] * lagged - moments[1] * mode_state, axis=2)
        gram_acc = gram_acc + jnp.einsum("tgm,sgm->gts", e_block, z_wide, precision=precise)
        fresh_part = jnp.einsum("kgns,sgm->kngm", block_ends, z_wide, precision=threepass)
        new_lagged = block_span * lagged - block_len * block_span * mode_state + fresh_part[1]
        new_state = block_span * mode_state + fresh_part[0]
        return ((new_state, new_lagged, first_acc, lag_acc, gram_acc), inside_part + carried)

    zero_state = jnp.zeros((order_count, group_count, members), jnp.float32)
    zero_pairs = jnp.zeros((order_count, group_count), jnp.float32)
    zero_gram = jnp.zeros((group_count, block_len, block_len), jnp.float32)
    final_carry, inner_blocks = lax.scan(
        forward_block,
        (zero_state, zero_state, zero_pairs, zero_pairs, zero_gram),
        (z_blocks, e_blocks),
    )
    first_acc, lag_acc, gram_acc = (final_carry[2], final_carry[3], final_carry[4])

    def backward_block(later_state, e_block):
        inside_part = jnp.einsum("gts,tgm->sgm", toeplitz, e_block, precision=precise)
        carried = jnp.einsum("gns,ngm->sgm", coef_tail, later_state, precision=precise)
        fresh_part = jnp.einsum("gnt,tgm->ngm", block_pow, e_block, precision=precise)
        return (block_span * later_state + fresh_part, inside_part + carried)

    top_state, grad_blocks = lax.scan(backward_block, zero_state, e_blocks, reverse=True)
    prev_grouped = prev_state.reshape(order_count, group_count, members)
    lagged_grouped = prev_lagged.reshape(order_count, group_count, members)
    next_grouped = next_state.reshape(order_count, group_count, members)
    device_after = decay_from * jnp.exp(-rate_axis)
    inner_sum = inner_blocks.reshape(tokens, group_count, members) + jnp.einsum(
        "gnt,ngm->tgm", mode_coefs[:, :, None] * device_after, prev_grouped, precision=precise
    )
    first_moment = jnp.exp(-decay_rates).T[:, :, None] * start_state
    second_moment = jnp.einsum(
        "gnt,tgm->ngm", (positions + 1.0) * device_after, grouped_e, precision=precise
    )
    first_acc = first_acc + jnp.sum(first_moment * prev_grouped, axis=2)
    lag_acc = lag_acc + jnp.sum(
        first_moment * lagged_grouped - second_moment * prev_grouped, axis=2
    )
    device_tail = mode_coefs[:, :, None] * jnp.flip(device_after, 2)
    product_grad = grad_blocks.reshape(tokens, group_count, members) + jnp.einsum(
        "gns,ngm->sgm", device_tail, next_grouped, precision=precise
    )
    lag_totals = diagonal_sums(gram_acc)
    first_total = first_acc.T + jnp.sum(lag_totals[:, None, :] * block_pow, axis=2)
    lag_total = lag_acc.T - jnp.sum(lag_totals[:, None, :] * lag_axis * block_pow, axis=2)
    gain_part = jnp.sqrt(2.0 * decay_rates) * first_total
    rate_part = mode_coefs * (0.5 * first_total + decay_rates * lag_total)
    inner_flat = inner_sum.reshape(tokens, channels)
    mixer_output = (query_part * inner_flat).astype(jnp.bfloat16)
    grad_flat = product_grad.reshape(tokens, channels)
    feature_adj = jnp.stack([cotangent * inner_flat, grad_flat * value_part, grad_flat * key_part])
    later_rows = passed_along(feature_adj[:, :rim_rows, :], "ctx", -1)
    appended = jnp.concatenate([feature_adj, later_rows], axis=1)
    feature_grads = short_conv(short_taps, appended, tokens, rim_rows, False).astype(jnp.bfloat16)
    filter_local = jnp.stack([gain_part, rate_part])
    entry_count = 2 * group_count * order_count * lax.axis_size("fsdp")
    summed = lax.psum(filter_local, "ctx")
    squares = lax.psum(jnp.sum(summed * summed), "fsdp")
    factor = jnp.minimum(1.0, lax.rsqrt(squares / entry_count + 1e-06))
    clipped = summed * factor
    return (mixer_output, feature_grads, clipped[0], clipped[1])


def solution(mesh):
    return jax.shard_map(
        per_device,
        mesh=mesh,
        in_specs=(
            P(None, "ctx", "fsdp"),
            P(None, None, "fsdp"),
            P("fsdp", None),
            P("fsdp", None),
            P("ctx", "fsdp"),
        ),
        out_specs=(P("ctx", "fsdp"), P(None, "ctx", "fsdp"), P("fsdp", None), P("fsdp", None)),
        check_vma=False,
    )
```

profile of v0, /device:TPU:1, one launch (start us, length us, event | category | flops | bytes accessed | tf_op | source)
XLA Modules:
  0.0 575.3 jit_solution(6784911890546579179)
XLA Ops:
  2.2 5.1 collective-permute-start
  14.9 54.5 %gather_fusion = f32[16384,16]{1,0:T(8,128)} fusion(f32[16,128]{0,1:T(8,128)S(1)} %copy.59, s32[16384]{0:T(1024)S(1)} %bitcast_clamp_fusion), kind=kCustom, calls=%fused_computation | custom fusion | bytes 2162688 | tf_op jit(solution)/shard_map/gather | solution.py:99
  69.4 5.2 copy.60
  77.4 2.6 copy.55
  80.0 3.3 rev.26
  87.9 4.8 multiply_add_fusion
  95.4 3.3 fusion.63
  105.0 41.3 %all_gather.3 = f32[16,3,16,256]{3,2,1,0:T(8,128)S(1)} all-gather(f32[1,3,16,256]{3,2,1,0:T(8,128)S(1)} %pad_maximum_fusion.5), channel_id=1, replica_groups=mesh['fsdp'=32,'ctx'=16] {'ctx'}, dimensions={0}, use_global_device_ids=true | all-gather | bytes 835584 | tf_op jit(solution)/shard_map/all_gather | solution.py:69
  154.0 132.3 %while.38 = (s32[]{:T(128)}, f32[16,16,16]{0,2,1:T(8,128)S(1)}, f32[16,16,16]{0,2,1:T(8,128)}, f32[16,16]{0,1:T(8,128)}, f32[16,16]{0,1:T(8,128)}, /*index=5*/f3...) while((s32[]{:T(128)}, f32[16,16,16]{0,2,1:T(8,128)S(1)}, ...), condition=%wide.region_4.5_spmd.clone, body=%wide.region_1.0_spmd.clone.sunk | while | flops 101380864 | bytes 5014714 | solution.py:121
  156.8 2.9 convolution_bitcast_fusion.8
  162.6 4.5 dynamic_update_slice.17
  172.0 2.9 convolution_bitcast_fusion.8
  179.4 4.5 dynamic_update_slice.17
  188.7 2.9 convolution_bitcast_fusion.8
  196.1 4.5 dynamic_update_slice.17
  205.5 2.9 convolution_bitcast_fusion.8
  212.9 4.5 dynamic_update_slice.17
  222.2 2.9 convolution_bitcast_fusion.8
  229.6 4.5 dynamic_update_slice.17
  239.0 2.9 convolution_bitcast_fusion.8
  246.3 4.5 dynamic_update_slice.17
  255.7 2.9 convolution_bitcast_fusion.8
  263.1 4.5 dynamic_update_slice.17
  272.5 2.9 convolution_bitcast_fusion.8
  279.8 4.5 dynamic_update_slice.17
  286.4 5.8 %rev.30 = f32[16,128,128]{2,1,0:T(8,128)} reverse(f32[16,128,128]{2,1,0:T(8,128)S(1)} %get-tuple-element.242), dimensions={2} | reverse | bytes 2097152 | tf_op jit(solution)/shard_map/jit(_flip)/rev | solution.py:18
  296.3 6.3 %reshape.172 = f32[16,128,255]{2,1,0:T(8,128)} reshape(f32[16,32640]{1,0:T(8,128)} %slice.116) | data formatting | bytes 4177920 | tf_op jit(solution)/shard_map/reshape | solution.py:23
  302.6 2.4 reduce_sum.112
  307.9 2.6 fusion.68
  311.3 61.1 %psum.14 = f32[2,16,16]{2,1,0:T(8,128)S(1)} all-reduce(f32[2,16,16]{2,1,0:T(8,128)S(1)} %pad_maximum_fusion.6), channel_id=1, replica_groups=mesh['fsdp'=32,'ctx'=16] {'ctx'}, use_global_device_ids=true, to_apply=%region_15.16 | all-reduce | flops 512 | bytes 4096 | tf_op jit(solution)/shard_map/psum | solution.py:168
  373.0 5.5 rev.29
  378.5 108.7 %psum.15 = f32[]{:T(128)} all-reduce(f32[]{:T(128)} %multiply_reduce_fusion.6), channel_id=1, replica_groups=mesh['fsdp'=32,'ctx'=16] {'fsdp'}, use_global_device_ids=true, to_apply=%region_17.18 | all-reduce | flops 1 | bytes 8 | tf_op jit(solution)/shard_map/psum | solution.py:169
  491.4 49.0 %while.39 = (s32[]{:T(128)}, f32[16,16,16]{0,2,1:T(8,128)S(1)}, f32[8,128,16,16]{1,0,3,2:T(8,128)}, f32[16,16,1]{0,1,2:T(8,128)S(1)}, f32[8,128,16,16]{1,3,2,0:T...) while((s32[]{:T(128)}, f32[16,16,16]{0,2,1:T(8,128)S(1)}, ...), condition=%wide.region_7.8_spmd.clone, body=%wide.region_6.7_spmd.clone.sunk | while | flops 62996484 | bytes 2277520 | solution.py:134
  492.6 4.5 dynamic_update_slice.18
  498.8 4.5 dynamic_update_slice.18
  504.9 4.5 dynamic_update_slice.18
  511.0 4.5 dynamic_update_slice.18
  517.2 4.5 dynamic_update_slice.18
  523.3 4.5 dynamic_update_slice.18
  529.4 4.5 dynamic_update_slice.18
  535.5 4.5 dynamic_update_slice.18
  540.4 2.5 reshape.168
  543.0 2.6 fusion.61
  547.3 2.4 reshape.164
  549.6 2.6 fusion.62
  558.4 9.5 %collective-permute-done.1 = f32[3,2,256]{1,2,0:T(8,128)S(1)} collective-permute-done((f32[3,2,256]{1,2,0:T(8,128)S(1)}, f32[3,2,256]{1,2,0:T(8,128)S(1)}, u32[]{:S(2)}, u32[]{:S(2)}) %collective-permute-start.1) | collective-permute-done | bytes 6176 | tf_op jit(solution)/shard_map/ppermute | solution.py:13
  569.5 3.3 fusion.54
  572.8 2.6 copy.77
  (215 shorter events, 140.8 us)
Async XLA Ops:
  2.2 85.7 %collective-permute-start = (bf16[3,2,256]{1,2,0:T(8,128)(2,1)}, bf16[3,2,256]{1,2,0:T(8,128)(2,1)}, u32[]{:S(2)}, u32[]{:S(2)}) collective-permute-start(bf16[3,2,256]{1,2,0:T(8,128)(2,1)} %copy.56), channel_id=1, source_target_pairs={{0,1},{1,2},{2,3},{3,4},{4,5},{5,6},{6,7},{7,8},{8,9},{9,10},{10,1... | collective-permute-start | bytes 9224 | tf_op jit(solution)/shard_map/ppermute | solution.py:13
  10.3 4.0 copy-start.19
  10.3 4.3 copy-start.17
  10.3 3.4 copy-start.29
  76.7 6.5 %copy-start.28 = (f32[3,1,256]{2,1,0:T(1,128)S(1)}, f32[3,1,256]{2,1,0:T(1,128)}, u32[]{:S(2)}) copy-start(f32[3,1,256]{2,1,0:T(1,128)} %get-tuple-element.483) | copy-start | bytes 9220
  77.4 7.9 %copy-start.27 = (f32[16,16]{0,1:T(8,128)S(1)}, f32[16,16]{0,1:T(8,128)}, u32[]{:S(2)}) copy-start(f32[16,16]{0,1:T(8,128)} %get-tuple-element.489) | copy-start | bytes 3076
  83.2 4.6 copy-start.25
  92.7 1.6 copy-start
  92.7 2.6 copy-start.10
  92.7 2.7 copy-start.11
  102.1 49.1 %copy-start.8 = (f32[1024,256]{0,1:T(8,128)}, f32[1024,256]{0,1:T(8,128)S(1)}, u32[]{:S(2)}) copy-start(f32[1024,256]{0,1:T(8,128)S(1)} %convert_multiply_fusion.1) | copy-start | bytes 3145732
  103.6 47.8 %copy-start.15 = (f32[16,16,16]{2,1,0:T(8,128)}, f32[16,16,16]{2,1,0:T(8,128)S(1)}, u32[]{:S(2)}) copy-start(f32[16,16,16]{2,1,0:T(8,128)S(1)} %fusion.75) | copy-start | bytes 49156
  150.9 1.0 copy-start.12
  296.3 10.9 %copy-start.14 = (f32[16,256]{0,1:T(8,128)S(1)}, f32[16,256]{0,1:T(8,128)}, u32[]{:S(2)}) copy-start(f32[16,256]{0,1:T(8,128)} %copy.70) | copy-start | bytes 49156
  296.3 10.9 %copy-start.16 = (f32[16,16,16]{2,1,0:T(8,128)S(1)}, f32[16,16,16]{2,1,0:T(8,128)}, u32[]{:S(2)}) copy-start(f32[16,16,16]{2,1,0:T(8,128)} %copy-done.15) | copy-start | bytes 49156
  296.3 11.6 %copy-start.9 = (f32[1024,256]{0,1:T(8,128)S(1)}, f32[1024,256]{0,1:T(8,128)}, u32[]{:S(2)}) copy-start(f32[1024,256]{0,1:T(8,128)} %copy-done.8) | copy-start | bytes 3145732
  491.4 51.5 %copy-start.21 = (f32[16,256]{1,0:T(8,128)S(1)}, f32[16,256]{1,0:T(8,128)}, u32[]{:S(2)}) copy-start(f32[16,256]{1,0:T(8,128)} %get-tuple-element.414) | copy-start | bytes 49156
  491.4 51.6 %copy-start.20 = (f32[16,16]{1,0:T(8,128)S(1)}, f32[16,16]{1,0:T(8,128)}, u32[]{:S(2)}) copy-start(f32[16,16]{1,0:T(8,128)} %get-tuple-element.758) | copy-start | bytes 3076
  540.4 5.2 copy-start.1
  545.6 4.0 copy-start.18
  549.6 4.6 copy-start.2
  549.6 4.6 copy-start.4
  554.3 1.0 copy-start.6
  554.3 2.5 copy-start.22
  554.3 3.1 copy-start.13
  554.3 13.6 %copy-start.3 = (f32[1,1024,256]{1,2,0:T(8,128)S(1)}, f32[1,1024,256]{1,2,0:T(8,128)}, u32[]{:S(2)}) copy-start(f32[1,1024,256]{1,2,0:T(8,128)} %get-tuple-element.471) | copy-start | bytes 3145732
  554.3 13.6 %copy-start.5 = (f32[1,1024,256]{1,2,0:T(8,128)S(1)}, f32[1,1024,256]{1,2,0:T(8,128)}, u32[]{:S(2)}) copy-start(f32[1,1024,256]{1,2,0:T(8,128)} %get-tuple-element.472) | copy-start | bytes 3145732
  555.4 12.6 %collective-permute-start.1 = (f32[3,2,256]{1,2,0:T(8,128)S(1)}, f32[3,2,256]{1,2,0:T(8,128)S(1)}, u32[]{:S(2)}, u32[]{:S(2)}) collective-permute-start(f32[3,2,256]{1,2,0:T(8,128)S(1)} %slice.113), channel_id=1, source_target_pairs={{1,0},{2,1},{3,2},{4,3},{5,4},{6,5},{7,6},{8,7},{9,8},{10,9},{11,1... | collective-permute-start | bytes 18440 | tf_op jit(solution)/shard_map/ppermute | solution.py:13
  558.4 11.0 %copy-start.7 = (f32[1,1024,256]{1,2,0:T(8,128)S(1)}, f32[1,1024,256]{1,2,0:T(8,128)}, u32[]{:S(2)}) copy-start(f32[1,1024,256]{1,2,0:T(8,128)} %copy-done.6) | copy-start | bytes 3145732
  558.4 11.0 %copy-start.23 = (f32[3,256]{1,0:T(4,128)S(1)}, f32[3,256]{1,0:T(4,128)}, u32[]{:S(2)}) copy-start(f32[3,256]{1,0:T(4,128)} %get-tuple-element.499) | copy-start | bytes 9220
  558.4 11.0 %copy-start.24 = (f32[3,256]{1,0:T(4,128)S(1)}, f32[3,256]{1,0:T(4,128)}, u32[]{:S(2)}) copy-start(f32[3,256]{1,0:T(4,128)} %get-tuple-element.500) | copy-start | bytes 9220
  558.4 11.0 %copy-start.26 = (f32[3,1,256]{2,0,1:T(4,128)S(1)}, f32[3,1,256]{2,0,1:T(4,128)}, u32[]{:S(2)}) copy-start(f32[3,1,256]{2,0,1:T(4,128)} %copy-done.25) | copy-start | bytes 9220
where the time goes:
time: 580 us; the launch traced here: 575 us
  blocking collectives  211 us (36%)
  local copies, waits for them, and re-layouts  189 us (33%)
  matrix products  99.5 us (17%)
  other arithmetic  57.1 us (10%)
  waiting for transfers between devices  9.53 us (2%)
  starting transfers between devices  6.47 us (1%)
    psum x1, blocking collectives, per_device(): squares = lax.psum(jnp.sum(summed * summed), 'fsdp')  109 us
    dynamic_update_slice x16, local copies, waits for them, and re-layouts, per_device(): lax.scan(forward_block, (zero_state, zero_state, zero_pairs, zero_pairs,...  71.3 us
    psum x1, blocking collectives, per_device(): summed = lax.psum(filter_local, 'ctx')  61.1 us
    gather x2, local copies, waits for them, and re-layouts, per_device(): filter_taps[:, jnp.maximum(lag_index, 0)]  59.7 us
    all_gather x1, blocking collectives, per_device(): everyone = lax.all_gather(local_states[None], 'ctx', axis=0, tiled=True)  41.3 us
    dot_general x8, matrix products, forward_block(): jnp.einsum('kgnt,tgm->kngm', block_moments, e_block, precision=precise)  23.1 us
    dot_general x8, matrix products, forward_block(): jnp.einsum('tgm,sgm->gts', e_block, z_wide, precision=precise)  16.3 us
    unnamed x72, local copies, waits for them, and re-layouts  15.9 us
  transfers between devices with their start and end apart: 2, of which 1 were waited for; matrix products, arithmetic and copies ran while one was open for 14% of the time, Pallas kernels for 0%

commit v1 on v0

--- a/solution.py
+++ b/solution.py
@@ -5,6 +5,12 @@
 
 precise = lax.Precision.HIGHEST
 threepass = lax.Precision.HIGH
+
+
+def add_all(shard, axis):
+    shards = lax.all_gather(shard, axis, axis=0, tiled=False)
+    summed = shards.sum(axis=0)
+    return summed
 
 
 def passed_along(value, axis, steps):
@@ -165,7 +171,7 @@
     feature_grads = short_conv(short_taps, appended, tokens, rim_rows, False).astype(jnp.bfloat16)
     filter_local = jnp.stack([gain_part, rate_part])
     entry_count = 2 * group_count * order_count * lax.axis_size("fsdp")
-    summed = lax.psum(filter_local, "ctx")
+    summed = add_all(filter_local, "ctx")
     squares = lax.psum(jnp.sum(summed * summed), "fsdp")
     factor = jnp.minimum(1.0, lax.rsqrt(squares / entry_count + 1e-06))
     clipped = summed * factor

time: 580 us -> 544 us (0.938)
  blocking collectives: 211 us -> 175 us
    psum x1 -> x0, blocking collectives: 61.1 us -> none  [per_device(): summed = lax.psum(filter_local, 'ctx')]
    all_gather x0 -> x1, blocking collectives: none -> 32.1 us  [add_all(): shards = lax.all_gather(shard, axis, axis=0, tiled=False)]
    psum x1, blocking collectives: 109 us -> 102 us  [per_device(): squares = lax.psum(jnp.sum(summed * summed), 'fsdp')]
    unnamed x72 -> x77, local copies, waits for them, and re-layouts: 15.9 us -> 17.3 us
  transfers between devices with their start and end apart: 2 -> 2, of which waited for: 1 -> 1; matrix products, arithmetic and copies ran while one was open for 14% -> 15% of each run, Pallas kernels for 0% -> 0%
where the time goes in v1:
time: 544 us; the launch traced here: 540 us
  local copies, waits for them, and re-layouts  190 us (35%)
  blocking collectives  175 us (32%)
  matrix products  99.5 us (18%)
  other arithmetic  56.3 us (10%)
  waiting for transfers between devices  9.4 us (2%)
  starting transfers between devices  6.47 us (1%)
    psum x1, blocking collectives, per_device(): squares = lax.psum(jnp.sum(summed * summed), 'fsdp')  102 us
    dynamic_update_slice x16, local copies, waits for them, and re-layouts, per_device(): lax.scan(forward_block, (zero_state, zero_state, zero_pairs, zero_pairs,...  71.3 us
    gather x2, local copies, waits for them, and re-layouts, per_device(): filter_taps[:, jnp.maximum(lag_index, 0)]  60 us
    all_gather x1, blocking collectives, per_device(): everyone = lax.all_gather(local_states[None], 'ctx', axis=0, tiled=True)  41.3 us
    all_gather x1, blocking collectives, add_all(): shards = lax.all_gather(shard, axis, axis=0, tiled=False)  32.1 us
    dot_general x8, matrix products, forward_block(): jnp.einsum('kgnt,tgm->kngm', block_moments, e_block, precision=precise)  23.1 us
    unnamed x77, local copies, waits for them, and re-layouts  17.3 us
    dot_general x8, matrix products, forward_block(): jnp.einsum('tgm,sgm->gts', e_block, z_wide, precision=precise)  16.3 us
  transfers between devices with their start and end apart: 2, of which 1 were waited for; matrix products, arithmetic and copies ran while one was open for 15% of the time, Pallas kernels for 0%

profile of v1, /device:TPU:1, one launch (start us, length us, event | category | flops | bytes accessed | tf_op | source)
XLA Modules:
  0.0 539.8 jit_solution(11838689247109927772)
XLA Ops:
  2.2 5.0 collective-permute-start
  14.9 54.8 %gather_fusion = f32[16384,16]{1,0:T(8,128)} fusion(f32[16,128]{0,1:T(8,128)S(1)} %copy.67, s32[16384]{0:T(1024)S(1)} %bitcast_clamp_fusion), kind=kCustom, calls=%fused_computation | custom fusion | bytes 2162688 | tf_op jit(solution)/shard_map/gather | solution.py:105
  69.7 5.2 copy.68
  77.6 2.6 copy.63
  80.2 3.3 rev.26
  88.1 4.7 multiply_add_fusion
  95.5 3.3 fusion.63
  105.1 41.3 %all_gather.9 = f32[16,3,16,256]{3,2,1,0:T(8,128)S(1)} all-gather(f32[1,3,16,256]{3,2,1,0:T(8,128)S(1)} %pad_maximum_fusion.5), channel_id=1, replica_groups=mesh['fsdp'=32,'ctx'=16] {'ctx'}, dimensions={0}, use_global_device_ids=true | all-gather | bytes 835584 | tf_op jit(solution)/shard_map/all_gather | solution.py:75
  154.1 132.3 %while.38 = (s32[]{:T(128)}, f32[16,16,16]{0,2,1:T(8,128)S(1)}, f32[16,16,16]{0,2,1:T(8,128)}, f32[16,16]{0,1:T(8,128)}, f32[16,16]{0,1:T(8,128)}, /*index=5*/f3...) while((s32[]{:T(128)}, f32[16,16,16]{0,2,1:T(8,128)S(1)}, ...), condition=%wide.region_4.5_spmd.clone, body=%wide.region_1.0_spmd.clone.sunk | while | flops 101380864 | bytes 5014714 | solution.py:127
  156.9 2.9 convolution_bitcast_fusion.8
  162.7 4.5 dynamic_update_slice.17
  172.1 2.9 convolution_bitcast_fusion.8
  179.5 4.5 dynamic_update_slice.17
  188.8 2.9 convolution_bitcast_fusion.8
  196.2 4.5 dynamic_update_slice.17
  205.6 2.9 convolution_bitcast_fusion.8
  213.0 4.5 dynamic_update_slice.17
  222.3 2.9 convolution_bitcast_fusion.8
  229.7 4.5 dynamic_update_slice.17
  239.1 2.9 convolution_bitcast_fusion.8
  246.4 4.5 dynamic_update_slice.17
  255.8 2.9 convolution_bitcast_fusion.8
  263.2 4.5 dynamic_update_slice.17
  272.5 2.9 convolution_bitcast_fusion.8
  279.9 4.5 dynamic_update_slice.17
  286.5 5.8 %rev.30 = f32[16,128,128]{2,1,0:T(8,128)} reverse(f32[16,128,128]{2,1,0:T(8,128)S(1)} %get-tuple-element.242), dimensions={2} | reverse | bytes 2097152 | tf_op jit(solution)/shard_map/jit(_flip)/rev | solution.py:24
  296.5 6.3 %reshape.172 = f32[16,128,255]{2,1,0:T(8,128)} reshape(f32[16,32640]{1,0:T(8,128)} %slice.116) | data formatting | bytes 4177920 | tf_op jit(solution)/shard_map/reshape | solution.py:29
  302.7 2.4 reduce_sum.121
  308.1 2.6 fusion.68
  311.5 32.1 %all-gather = f32[32,16,16]{2,1,0:T(8,128)S(1)} all-gather(f32[2,16,16]{2,1,0:T(8,128)S(1)} %pad_maximum_fusion.6), channel_id=2, replica_groups=mesh['fsdp'=32,'ctx'=16] {'ctx'}, dimensions={0}, use_global_device_ids=true | all-gather | bytes 34816 | tf_op jit(solution)/shard_map/all_gather | solution.py:11
  344.3 5.5 %rev.29 = f32[16,16,1024]{2,1,0:T(8,128)} reverse(f32[16,16,1024]{2,1,0:T(8,128)} %get-tuple-element.493), dimensions={2} | reverse | bytes 2097152 | tf_op jit(solution)/shard_map/jit(_flip)/rev | solution.py:156
  349.8 102.0 %psum.7 = f32[]{:T(128)} all-reduce(f32[]{:T(128)} %multiply_reduce_fusion.6), channel_id=1, replica_groups=mesh['fsdp'=32,'ctx'=16] {'fsdp'}, use_global_device_ids=true, to_apply=%region_17.18 | all-reduce | flops 1 | bytes 8 | tf_op jit(solution)/shard_map/psum | solution.py:175
  455.3 48.9 %while.39 = (s32[]{:T(128)}, f32[16,16,16]{0,2,1:T(8,128)S(1)}, f32[8,128,16,16]{1,0,3,2:T(8,128)}, f32[16,16,1]{0,1,2:T(8,128)S(1)}, f32[8,128,16,16]{1,3,2,0:T...) while((s32[]{:T(128)}, f32[16,16,16]{0,2,1:T(8,128)S(1)}, ...), condition=%wide.region_7.8_spmd.clone, body=%wide.region_6.7_spmd.clone.sunk | while | flops 62996484 | bytes 2277520 | solution.py:140
  456.5 4.5 dynamic_update_slice.18
  462.6 4.5 dynamic_update_slice.18
  468.7 4.5 dynamic_update_slice.18
  474.9 4.5 dynamic_update_slice.18
  481.0 4.5 dynamic_update_slice.18
  487.1 4.5 dynamic_update_slice.18
  493.2 4.5 dynamic_update_slice.18
  499.4 4.5 dynamic_update_slice.18
  504.2 2.5 reshape.168
  506.8 2.6 fusion.61
  511.1 2.4 reshape.164
  513.5 2.6 fusion.62
  523.0 9.4 %collective-permute-done.1 = f32[3,2,256]{1,2,0:T(8,128)S(1)} collective-permute-done((f32[3,2,256]{1,2,0:T(8,128)S(1)}, f32[3,2,256]{1,2,0:T(8,128)S(1)}, u32[]{:S(2)}, u32[]{:S(2)}) %collective-permute-start.1) | collective-permute-done | bytes 6176 | tf_op jit(solution)/shard_map/ppermute | solution.py:19
  533.9 3.3 fusion.54
  537.2 2.6 copy.86
  (221 shorter events, 140.9 us)
Async XLA Ops:
  2.2 85.9 %collective-permute-start = (bf16[3,2,256]{1,2,0:T(8,128)(2,1)}, bf16[3,2,256]{1,2,0:T(8,128)(2,1)}, u32[]{:S(2)}, u32[]{:S(2)}) collective-permute-start(bf16[3,2,256]{1,2,0:T(8,128)(2,1)} %copy.64), channel_id=1, source_target_pairs={{0,1},{1,2},{2,3},{3,4},{4,5},{5,6},{6,7},{7,8},{8,9},{9,10},{10,1... | collective-permute-start | bytes 9224 | tf_op jit(solution)/shard_map/ppermute | solution.py:19
  10.3 4.0 copy-start.19
  10.3 4.3 copy-start.17
  10.3 3.4 copy-start.30
  77.1 6.4 %copy-start.29 = (f32[3,1,256]{2,1,0:T(1,128)S(1)}, f32[3,1,256]{2,1,0:T(1,128)}, u32[]{:S(2)}) copy-start(f32[3,1,256]{2,1,0:T(1,128)} %get-tuple-element.483) | copy-start | bytes 9220
  77.6 8.0 %copy-start.28 = (f32[16,16]{0,1:T(8,128)S(1)}, f32[16,16]{0,1:T(8,128)}, u32[]{:S(2)}) copy-start(f32[16,16]{0,1:T(8,128)} %get-tuple-element.489) | copy-start | bytes 3076
  83.5 4.6 copy-start.26
  92.8 1.6 copy-start
  92.8 2.6 copy-start.10
  92.8 2.7 copy-start.11
  102.2 49.0 %copy-start.8 = (f32[1024,256]{0,1:T(8,128)}, f32[1024,256]{0,1:T(8,128)S(1)}, u32[]{:S(2)}) copy-start(f32[1024,256]{0,1:T(8,128)S(1)} %convert_multiply_fusion.1) | copy-start | bytes 3145732
  103.7 47.7 %copy-start.15 = (f32[16,16,16]{2,1,0:T(8,128)}, f32[16,16,16]{2,1,0:T(8,128)S(1)}, u32[]{:S(2)}) copy-start(f32[16,16,16]{2,1,0:T(8,128)S(1)} %fusion.75) | copy-start | bytes 49156
  151.0 1.0 copy-start.12
  296.4 10.9 %copy-start.14 = (f32[16,256]{0,1:T(8,128)S(1)}, f32[16,256]{0,1:T(8,128)}, u32[]{:S(2)}) copy-start(f32[16,256]{0,1:T(8,128)} %copy.78) | copy-start | bytes 49156
  296.4 10.9 %copy-start.16 = (f32[16,16,16]{2,1,0:T(8,128)S(1)}, f32[16,16,16]{2,1,0:T(8,128)}, u32[]{:S(2)}) copy-start(f32[16,16,16]{2,1,0:T(8,128)} %copy-done.15) | copy-start | bytes 49156
  296.5 11.6 %copy-start.9 = (f32[1024,256]{0,1:T(8,128)S(1)}, f32[1024,256]{0,1:T(8,128)}, u32[]{:S(2)}) copy-start(f32[1024,256]{0,1:T(8,128)} %copy-done.8) | copy-start | bytes 3145732
  310.7 143.4 %copy-start.20 = (f32[16,16]{1,0:T(8,128)S(1)}, f32[16,16]{1,0:T(8,128)}, u32[]{:S(2)}) copy-start(f32[16,16]{1,0:T(8,128)} %get-tuple-element.758) | copy-start | bytes 3076
  455.3 51.5 %copy-start.22 = (f32[16,256]{1,0:T(8,128)S(1)}, f32[16,256]{1,0:T(8,128)}, u32[]{:S(2)}) copy-start(f32[16,256]{1,0:T(8,128)} %get-tuple-element.414) | copy-start | bytes 49156
  455.3 51.6 %copy-start.21 = (f32[16,16]{1,0:T(8,128)S(1)}, f32[16,16]{1,0:T(8,128)}, u32[]{:S(2)}) copy-start(f32[16,16]{1,0:T(8,128)} %get-tuple-element.758) | copy-start | bytes 3076
  504.2 5.2 copy-start.1
  509.4 4.0 copy-start.18
  513.5 4.6 copy-start.2
  513.5 4.6 copy-start.4
  518.1 1.0 copy-start.6
  518.1 2.5 copy-start.23
  518.1 3.9 copy-start.13
  518.1 14.3 %copy-start.3 = (f32[1,1024,256]{1,2,0:T(8,128)S(1)}, f32[1,1024,256]{1,2,0:T(8,128)}, u32[]{:S(2)}) copy-start(f32[1,1024,256]{1,2,0:T(8,128)} %get-tuple-element.471) | copy-start | bytes 3145732
  518.1 14.3 %copy-start.5 = (f32[1,1024,256]{1,2,0:T(8,128)S(1)}, f32[1,1024,256]{1,2,0:T(8,128)}, u32[]{:S(2)}) copy-start(f32[1,1024,256]{1,2,0:T(8,128)} %get-tuple-element.472) | copy-start | bytes 3145732
  519.2 13.2 %collective-permute-start.1 = (f32[3,2,256]{1,2,0:T(8,128)S(1)}, f32[3,2,256]{1,2,0:T(8,128)S(1)}, u32[]{:S(2)}, u32[]{:S(2)}) collective-permute-start(f32[3,2,256]{1,2,0:T(8,128)S(1)} %slice.113), channel_id=1, source_target_pairs={{1,0},{2,1},{3,2},{4,3},{5,4},{6,5},{7,6},{8,7},{9,8},{10,9},{11,1... | collective-permute-start | bytes 18440 | tf_op jit(solution)/shard_map/ppermute | solution.py:19
  523.0 10.9 %copy-start.7 = (f32[1,1024,256]{1,2,0:T(8,128)S(1)}, f32[1,1024,256]{1,2,0:T(8,128)}, u32[]{:S(2)}) copy-start(f32[1,1024,256]{1,2,0:T(8,128)} %copy-done.6) | copy-start | bytes 3145732
  523.0 10.9 %copy-start.24 = (f32[3,256]{1,0:T(4,128)S(1)}, f32[3,256]{1,0:T(4,128)}, u32[]{:S(2)}) copy-start(f32[3,256]{1,0:T(4,128)} %get-tuple-element.499) | copy-start | bytes 9220
  523.0 10.9 %copy-start.25 = (f32[3,256]{1,0:T(4,128)S(1)}, f32[3,256]{1,0:T(4,128)}, u32[]{:S(2)}) copy-start(f32[3,256]{1,0:T(4,128)} %get-tuple-element.500) | copy-start | bytes 9220
  523.0 10.9 %copy-start.27 = (f32[3,1,256]{2,0,1:T(4,128)S(1)}, f32[3,1,256]{2,0,1:T(4,128)}, u32[]{:S(2)}) copy-start(f32[3,1,256]{2,0,1:T(4,128)} %copy-done.26) | copy-start | bytes 9220
